TPU v7x, 128 devices: a whole 4x4x4 slice. The times are simulated.
128 devices in a mesh: lon: 8 (over y_lo, z), lat: 16 (over y_hi, x, core).
Axes of the slice: x: 4, y: 4 (y_hi: 2, y_lo: 2; y = y_hi * 2 + y_lo), z: 4, core: 2. Of those that a mesh axis runs over, the one named last changes fastest.
Arguments:
- costate: float32 [72, 8, 128, 2048], P(None, None, 'lat', 'lon'), may hold values from -6 to 6
- diffusion: float32 [2, 71, 128, 2048], P(None, None, 'lat', 'lon'), may hold values from 0.025 to 400
- east_courant: float32 [2, 128, 2048], P(None, 'lat', 'lon'), may hold values from 0.05 to 0.9
- north_courant: float32 [2, 128, 2048], P(None, 'lat', 'lon'), may hold values from 0.02 to 0.45
- south_courant: float32 [2, 128, 2048], P(None, 'lat', 'lon'), may hold values from 0.02 to 0.45
- polar_shift: int32 [2, 128], replicated, may hold values from -1024 to 1024
- owners: int32 [2, 163840, 1], P(None, ('lon', 'lat')), may hold values from 0 to 127; in each aligned block of 1280 rows (0 to 1279, 1280 to 2559, ..., all dimensions but the last counted through in order) at most 16 rows name the same one
- columns: int32 [2, 163840], P(None, ('lon', 'lat')), may hold values from 0 to 2047
- sounding_counts: int32 [2, 128], P(None, ('lon', 'lat')), may hold values from 640 to 1280, as said below
- kernels: float32 [2, 72, 163840], P(None, None, ('lon', 'lat')), may hold values from 0.1 to 2
- misfits: float32 [2, 8, 163840], P(None, None, ('lon', 'lat')), may hold values from -6 to 6
Outputs:
- adjoint_state: float32 [72, 8, 128, 2048], P(None, None, 'lat', 'lon')
- flux_gradient: float32 [8, 128, 2048], P(None, 'lat', 'lon')
Inputs may be any that keep to these rules, and one draw needn't show every extreme that they name: `owners`: in every step no owner is named by more than 16 of one device's 1280 soundings, and in every step some owner is named by exactly 16 of some device's soundings. `sounding_counts`: in every step some device is full and some holds exactly 640 live soundings.
All inputs are finite; a program needn't handle non-finite values.
Results may differ from a plain program's by a relative error of at most 0.0001.
Values sent between devices are 32-bit elements; how exact they have to be, the bound alone decides.
No kernel may reach another device: no remote copies, remote signals or barrier semaphores. Data moves between devices by JAX's collectives and lax.ppermute only.
A program may use at most 128 MiB of HBM per device.

v0:
```python
import functools

import jax
import jax.numpy as jnp
from jax import lax
from jax.experimental import pallas as pl
from jax.experimental.pallas import tpu as pltpu
from jax.sharding import PartitionSpec as P

AXES = ("lon", "lat")
LANES = 128
CAP = 16
GROUP = 8
F32 = jnp.float32
BF16 = jnp.bfloat16
VMEM_LIMIT = 56 * 1024 * 1024


def vmem():
    return pl.BlockSpec(memory_space=pltpu.VMEM)


def smem():
    return pl.BlockSpec(memory_space=pltpu.SMEM)


def params():
    return pltpu.CompilerParams(vmem_limit_bytes=VMEM_LIMIT)


def dot(a, b, contract=((1,), (0,))):
    return lax.dot_general(a, b, (contract, ((), ())), preferred_element_type=F32)


def halves(x):
    high = x.astype(BF16)
    return high, (x - high.astype(F32)).astype(BF16)


def pack_kernel(step, counts, owners, columns, kernels, misfits, out, payload, target):
    held = owners.shape[2]
    owner = owners[step]
    live = lax.broadcasted_iota(jnp.int32, owner.shape, 1) < counts[step, 0]
    owner = jnp.where(live, owner, -1)
    shape = (LANES, LANES)
    device = lax.broadcasted_iota(jnp.int32, shape, 0)
    earlier = (device < lax.broadcasted_iota(jnp.int32, shape, 1)).astype(F32)
    table = jnp.concatenate([earlier, jnp.ones(shape, F32)], axis=1).astype(BF16)
    seen = jnp.zeros(shape, F32)
    for start in range(0, held, LANES):
        here = owner[:, start : start + LANES]
        hot = device == here
        counted = dot(jnp.where(hot, 1.0, 0.0).astype(BF16), table)
        rank = jnp.sum(
            jnp.where(hot, counted[:, :LANES] + seen, 0.0), axis=0, keepdims=True
        )
        seen = seen + counted[:, LANES:]
        target[:, start : start + LANES] = jnp.where(
            here >= 0, here * CAP + rank.astype(jnp.int32), -1
        )
    levels, tracers = kernels.shape[1], misfits.shape[1]
    fields = levels + tracers
    column = columns[step : step + 1, :].astype(F32) + 1.0
    column = jnp.where(lax.broadcasted_iota(jnp.int32, (8, held), 0) == 0, column, 0.0)
    rows = jnp.concatenate(
        [kernels[0], misfits[0], column, jnp.zeros((LANES - fields - 8, held), F32)], axis=0
    )
    high, low = halves(rows)
    payload[:LANES, :] = high
    payload[LANES:, :] = low
    block = 256

    def place(i, carry):
        slot = lax.broadcasted_iota(jnp.int32, (block, held), 0) + i * block
        hot = jnp.where(slot == target[...], 1.0, 0.0).astype(BF16)
        both = dot(hot, payload[...], ((1,), (1,)))
        out[pl.ds(pl.multiple_of(i * block, block), block), :] = (
            both[:, :LANES] + both[:, LANES:]
        )
        return carry

    lax.fori_loop(0, out.shape[0] // block, place, 0)


def packed(step, counts, owners, columns, kernels, misfits):
    levels, held = kernels.shape[1:]
    tracers = misfits.shape[1]
    devices = lax.axis_size("lon") * lax.axis_size("lat")
    return pl.pallas_call(
        functools.partial(pack_kernel, step),
        grid=(1,),
        out_shape=jax.ShapeDtypeStruct((devices * CAP, LANES), F32),
        in_specs=[
            smem(),
            pl.BlockSpec(owners.shape, lambda i: (0, 0, 0)),
            pl.BlockSpec(columns.shape, lambda i: (0, 0)),
            pl.BlockSpec((1, levels, held), lambda i: (step, 0, 0)),
            pl.BlockSpec((1, tracers, held), lambda i: (step, 0, 0)),
        ],
        out_specs=pl.BlockSpec((devices * CAP, LANES), lambda i: (0, 0)),
        scratch_shapes=[
            pltpu.VMEM((2 * LANES, held), BF16),
            pltpu.VMEM((1, held), jnp.int32),
        ],
        compiler_params=params(),
        name="pack",
    )(counts, owners, columns, kernels, misfits)


def forcing_kernel(received, out, high, low, cell):
    levels, rows, tracers, cells = out.shape
    slots = received.shape[0]

    def outer(i, carry):
        at = pl.multiple_of(i * LANES, LANES)
        block = received[pl.ds(at, LANES), :]
        turned = block.T
        cell[pl.ds(at, LANES), :] = jnp.broadcast_to(
            block[:, levels + tracers : levels + tracers + 1] - 1.0, (LANES, LANES)
        )
        product = turned[:levels][:, None, :] * turned[levels : levels + tracers][None]
        first, second = halves(product.reshape(levels * tracers, LANES))
        high[:, pl.ds(at, LANES)] = first
        low[:, pl.ds(at, LANES)] = second
        return carry

    lax.fori_loop(0, slots // LANES, outer, 0)

    def place(row, carry):
        lane = lax.broadcasted_iota(jnp.int32, (1, LANES), 1)
        first = (lane + row * cells).astype(F32)
        hot = jnp.concatenate(
            [
                jnp.where(cell[...] == first + float(part * LANES), 1.0, 0.0).astype(BF16)
                for part in range(cells // LANES)
            ],
            axis=1,
        )
        total = dot(high[...], hot) + dot(low[...], hot)
        out[:, pl.ds(row, 1), :, :] = total.reshape(levels, 1, tracers, cells)
        return carry

    lax.fori_loop(0, rows, place, 0)


def forcing(received, levels, tracers, rows, cells):
    slots = received.shape[0]
    return pl.pallas_call(
        forcing_kernel,
        out_shape=jax.ShapeDtypeStruct((levels, rows, tracers, cells), F32),
        in_specs=[vmem()],
        out_specs=vmem(),
        scratch_shapes=[
            pltpu.VMEM((levels * tracers, slots), BF16),
            pltpu.VMEM((levels * tracers, slots), BF16),
            pltpu.VMEM((slots, LANES), F32),
        ],
        compiler_params=params(),
        name="forcing",
    )(received)


def pivots(level, levels, diffusion, carry):
    below, ratio = carry
    above = diffusion[0, level] if level is not None else jnp.zeros_like(below)
    inverse = 1.0 / (1.0 + below + above + below * ratio)
    return inverse, below * inverse, above, -above * inverse


def spread(x, row, tracers):
    return jnp.broadcast_to(x[row : row + 1, :], (tracers, x.shape[1]))


def eliminate(level, above, carry, rights, ratios):
    below, ratio, values = carry
    if above is None:
        above = jnp.zeros_like(below)
    inverse = 1.0 / (1.0 + below + above + below * ratio)
    lower = below * inverse
    ratio = -above * inverse
    ratios[level] = ratio
    tracers = rights[0].shape[0]
    fresh = [
        spread(inverse, r, tracers) * rights[r] + spread(lower, r, tracers) * values[r]
        for r in range(len(rights))
    ]
    return (above, ratio, fresh)


def substitute(diffused, ratios, north, south, east, first, last, polar):
    levels, rows, tracers, cells = diffused.shape
    lat = lax.axis_index("lat")
    at_start = lat == 0
    row = jnp.where(at_start, 0, rows - 1)
    picked_north = jnp.where(at_start, north[0, 0:1, :], north[0, rows - 1 : rows, :])
    picked_south = jnp.where(at_start, south[0, 0:1, :], south[0, rows - 1 : rows, :])
    own = jnp.broadcast_to(1.0 - picked_north - picked_south, (tracers, cells))
    side = jnp.broadcast_to(jnp.where(at_start, picked_north, picked_south), (tracers, cells))
    picked_east = jnp.where(at_start, east[0, 0:1, :], east[0, rows - 1 : rows, :])
    polar[levels] = jnp.broadcast_to(picked_east, (tracers, cells))

    def one(level, solved):
        first[level] = solved[0]
        last[level] = solved[rows - 1]
        polar[level] = own * jnp.where(at_start, solved[0], solved[rows - 1]) + side * jnp.where(
            at_start, solved[1], solved[rows - 2]
        )

    solved = [diffused[levels - 1, r] for r in range(rows)]
    one(levels - 1, solved)

    def back(level, solved):
        ratio = ratios[level]
        fresh = []
        for r in range(rows):
            value = diffused[level, r] - spread(ratio, r, tracers) * solved[r]
            diffused[level, r] = value
            fresh.append(value)
        one(level, fresh)
        return fresh

    def steps(i, solved):
        for j in range(GROUP - 1):
            solved = back(levels - 2 - i * (GROUP - 1) - j, solved)
        return solved

    full = (levels - 1) // (GROUP - 1)
    solved = lax.fori_loop(0, full, steps, solved)
    for level in range(levels - 2 - full * (GROUP - 1), -1, -1):
        solved = back(level, solved)


def first_kernel(costate, diffusion, north, south, east, diffused, first, last, polar, ratios):
    levels, tracers, rows, cells = costate.shape
    zero = jnp.zeros((rows, cells), F32)
    carry = (zero, zero, [jnp.zeros((tracers, cells), F32)] * rows)

    def forward(level, above, carry):
        rights = [costate[level, :, r, :] for r in range(rows)]
        carry = eliminate(level, above, carry, rights, ratios)
        for r in range(rows):
            diffused[level, r] = carry[2][r]
        return carry

    def group(i, carry):
        for j in range(GROUP):
            level = i * GROUP + j
            carry = forward(level, diffusion[0, level], carry)
        return carry

    carry = lax.fori_loop(0, levels // GROUP - 1, group, carry)
    for level in range(levels - GROUP, levels):
        carry = forward(level, diffusion[0, level] if level < levels - 1 else None, carry)
    substitute(diffused, ratios, north, south, east, first, last, polar)


def meridional(level, row, diffused, after, before, coefs):
    rows = diffused.shape[1]
    own, north, south = coefs
    up = diffused[level, row + 1] if row < rows - 1 else after[level]
    down = diffused[level, row - 1] if row > 0 else before[level]
    return own * diffused[level, row] + north * up + south * down


def edge_kernel(diffused, after, before, north, south, edge):
    levels, rows, tracers, cells = diffused.shape
    shape = (tracers, LANES)
    lane = lax.broadcasted_iota(jnp.int32, shape, 1)
    coefs = []
    for r in range(rows):
        n = jnp.broadcast_to(north[0, r : r + 1, :LANES], shape)
        s = jnp.broadcast_to(south[0, r : r + 1, :LANES], shape)
        coefs.append((1.0 - n - s, n, s))

    def group(i, carry):
        packed_edge = jnp.zeros(shape, F32)
        for j in range(GROUP):
            level = i * GROUP + j
            values = [diffused[level, r, :, :LANES] for r in range(rows)]
            values = [before[level, :, :LANES]] + values + [after[level, :, :LANES]]
            for r in range(rows):
                own, n, s = coefs[r]
                value = own * values[r + 1] + n * values[r + 2] + s * values[r]
                at = j * rows + r
                packed_edge = jnp.where(
                    lane == at, pltpu.roll(value, at, 1) if at else value, packed_edge
                )
        edge[i] = packed_edge
        return carry

    lax.fori_loop(0, levels // GROUP, group, 0)


def prepare_stencil(shift, step, north, south, east, polars, coefs, turned):
    rows, cells = north.shape[1:]
    tracers = coefs.shape[2]
    for r in range(rows):
        n = north[0, r : r + 1, :]
        s = south[0, r : r + 1, :]
        coefs[0, r] = jnp.broadcast_to(1.0 - n - s, (tracers, cells))
        coefs[1, r] = jnp.broadcast_to(n, (tracers, cells))
        coefs[2, r] = jnp.broadcast_to(s, (tracers, cells))
        coefs[3, r] = jnp.broadcast_to(east[0, r : r + 1, :], (tracers, cells))
    levels = turned.shape[0]
    lat = lax.axis_index("lat")
    last_lat = lax.axis_size("lat") - 1
    last_row = rows * lax.axis_size("lat") - 1

    def turn(low, high, amount):
        inner = lax.rem(amount + 2 * 2048, 2048) & (cells - 1)
        back = 2 * cells - inner
        weight = jnp.concatenate([low[levels], high[levels]], axis=1)

        def one(level, carry):
            row = jnp.concatenate([low[level], high[level]], axis=1)
            moved = row + weight * (pltpu.roll(row, 2 * cells - 1, 1) - row)
            turned[level] = pltpu.roll(moved, back, 1)[:, :cells]
            return carry

        lax.fori_loop(0, levels, one, 0, unroll=4)

    @pl.when(lat == 0)
    def _():
        turn(polars[0], polars[1], shift[step, 0])

    @pl.when(lat == last_lat)
    def _():
        turn(polars[2], polars[3], shift[step, last_row])


def transported(level, lane_at, diffused, after, before, edge_row, coefs, turned):
    rows, tracers, cells = diffused.shape[1:]
    lat = lax.axis_index("lat")
    last = lax.broadcasted_iota(jnp.int32, (tracers, cells), 1) == cells - 1
    result = []
    for r in range(rows):
        mer = meridional(level, r, diffused, after, before, [coefs[k, r] for k in range(3)])
        arrived = pltpu.roll(edge_row, LANES - 1 - (lane_at * rows + r), 1)
        arrived = jnp.concatenate([arrived] * (cells // LANES), axis=1)
        following = jnp.where(last, arrived, pltpu.roll(mer, cells - 1, 1))
        result.append(mer + coefs[3, r] * (following - mer))
    result[0] = jnp.where(lat == 0, turned[level], result[0])
    result[rows - 1] = jnp.where(
        lat == lax.axis_size("lat") - 1, turned[level], result[rows - 1]
    )
    return result


def middle_kernel(
    step,
    shift,
    diffused,
    after,
    before,
    edge,
    low0,
    high0,
    low1,
    high1,
    north,
    south,
    east,
    forced,
    diffusion,
    next_north,
    next_south,
    next_east,
    solved,
    first,
    last,
    polar,
    surface,
    coefs,
    turned,
    ratios,
):
    levels, rows, tracers, cells = diffused.shape
    prepare_stencil(shift, step, north, south, east, (low0, high0, low1, high1), coefs, turned)
    zero = jnp.zeros((rows, cells), F32)
    carry = (zero, zero, [jnp.zeros((tracers, cells), F32)] * rows)

    def forward(level, j, above, edge_row, carry):
        rights = transported(level, j, diffused, after, before, edge_row, coefs, turned)
        rights = [rights[r] + forced[level, r] for r in range(rows)]
        if isinstance(level, int) and level == levels - 1:
            for r in range(rows):
                surface[r] = rights[r]
        carry = eliminate(level, above, carry, rights, ratios)
        for r in range(rows):
            solved[level, r] = carry[2][r]
        return carry

    def group(i, carry):
        edge_row = edge[i]
        for j in range(GROUP):
            level = i * GROUP + j
            carry = forward(level, j, diffusion[0, level], edge_row, carry)
        return carry

    groups = levels // GROUP
    carry = lax.fori_loop(0, groups - 1, group, carry)
    edge_row = edge[groups - 1]
    for j in range(GROUP):
        level = levels - GROUP + j
        above = diffusion[0, level] if level < levels - 1 else None
        carry = forward(level, j, above, edge_row, carry)
    substitute(solved, ratios, next_north, next_south, next_east, first, last, polar)


def last_kernel(
    step,
    shift,
    diffused,
    after,
    before,
    edge,
    low0,
    high0,
    low1,
    high1,
    north,
    south,
    east,
    forced,
    surface,
    state,
    gradient,
    coefs,
    turned,
):
    levels, rows, tracers, cells = diffused.shape
    prepare_stencil(shift, step, north, south, east, (low0, high0, low1, high1), coefs, turned)

    def group(i, carry):
        edge_row = edge[i]
        for j in range(GROUP):
            level = i * GROUP + j
            values = transported(level, j, diffused, after, before, edge_row, coefs, turned)
            for r in range(rows):
                state[level, :, r, :] = values[r] + forced[level, r]
        return carry

    lax.fori_loop(0, levels // GROUP, group, 0)
    for r in range(rows):
        gradient[:, r, :] = surface[r] + state[levels - 1, :, r, :]


def step_block(array, step):
    shape = (1,) + array.shape[1:]
    return pl.BlockSpec(shape, lambda i: (step,) + (0,) * (len(shape) - 1))


def whole(array):
    return pl.BlockSpec(array.shape, lambda i: (0,) * len(array.shape))


def exchange(diffused, first, last, polar, north, south, shift, step):
    lat_count = lax.axis_size("lat")
    lon_count = lax.axis_size("lon")
    up = [(i, i + 1) for i in range(lat_count - 1)]
    down = [(j, i) for i, j in up]
    after = lax.ppermute(first, "lat", down)
    before = lax.ppermute(last, "lat", up)
    cells = north.shape[2]
    circle = cells * lon_count

    def route(lat, hops, row):
        pairs = [
            (((j + hops) % lon_count) * lat_count + lat, j * lat_count + lat)
            for j in range(lon_count)
        ]
        return lax.ppermute(row, AXES, pairs)

    polars = []
    for lat, row in ((0, 0), (lat_count - 1, shift.shape[1] - 1)):
        hops = jnp.mod(shift[step, row], circle) // cells
        polars += lax.switch(
            hops,
            [
                functools.partial(
                    lambda k, lat, x: [route(lat, k, x), route(lat, k + 1, x)], k, lat
                )
                for k in range(lon_count)
            ],
            polar,
        )
    levels, rows, tracers = diffused.shape[:3]
    edge = pl.pallas_call(
        edge_kernel,
        grid=(1,),
        out_shape=jax.ShapeDtypeStruct((levels // GROUP, tracers, LANES), F32),
        in_specs=[whole(diffused), whole(after), whole(before)]
        + [step_block(north, step)] * 2,
        out_specs=pl.BlockSpec((levels // GROUP, tracers, LANES), lambda i: (0, 0, 0)),
        compiler_params=params(),
        name="edge",
    )(diffused, after, before, north, south)
    west = [(i, (i - 1) % lon_count) for i in range(lon_count)]
    return after, before, lax.ppermute(edge, "lon", west), polars


def per_device(
    costate,
    diffusion,
    east_courant,
    north_courant,
    south_courant,
    polar_shift,
    owners,
    columns,
    sounding_counts,
    kernels,
    misfits,
):
    levels, tracers, rows, cells = costate.shape
    devices = lax.axis_size("lon") * lax.axis_size("lat")
    owner_rows = owners.reshape(owners.shape[0], 1, owners.shape[1])
    couplings = [north_courant, south_courant, east_courant]

    def exchanged(step):
        sent = packed(step, sounding_counts, owner_rows, columns, kernels, misfits)
        sent = sent.reshape(devices, CAP, LANES)
        return lax.all_to_all(sent, AXES, 0, 0, tiled=True).reshape(devices * CAP, LANES)

    got = {step: exchanged(step) for step in (1, 0)}
    forced = {step: forcing(got[step], levels, tracers, rows, cells) for step in (1, 0)}

    solved_shapes = [
        jax.ShapeDtypeStruct((levels, rows, tracers, cells), F32),
        jax.ShapeDtypeStruct((levels, tracers, cells), F32),
        jax.ShapeDtypeStruct((levels, tracers, cells), F32),
        jax.ShapeDtypeStruct((levels + 1, tracers, cells), F32),
    ]
    ratio_scratch = pltpu.VMEM((levels, rows, cells), F32)
    stencil_scratch = [
        pltpu.VMEM((4, rows, tracers, cells), F32),
        pltpu.VMEM((levels, tracers, cells), F32),
    ]
    diffused, first, last, polar = pl.pallas_call(
        first_kernel,
        grid=(1,),
        out_shape=solved_shapes,
        in_specs=[whole(costate)] + [step_block(x, 1) for x in [diffusion] + couplings],
        out_specs=[whole(x) for x in solved_shapes],
        scratch_shapes=[ratio_scratch],
        compiler_params=params(),
        name="first",
    )(costate, diffusion, *couplings)
    after, before, edge, polars = exchange(
        diffused, first, last, polar, north_courant, south_courant, polar_shift, 1
    )
    surface_shape = jax.ShapeDtypeStruct((rows, tracers, cells), F32)
    operands = [diffused, after, before, edge, *polars]
    solved, first, last, polar, surface = pl.pallas_call(
        functools.partial(middle_kernel, 1),
        grid=(1,),
        out_shape=solved_shapes + [surface_shape],
        in_specs=[smem()]
        + [whole(x) for x in operands]
        + [step_block(x, 1) for x in couplings]
        + [whole(forced[1])]
        + [step_block(x, 0) for x in [diffusion] + couplings],
        out_specs=[whole(x) for x in solved_shapes + [surface_shape]],
        scratch_shapes=stencil_scratch + [ratio_scratch],
        compiler_params=params(),
        name="middle",
    )(polar_shift, *operands, *couplings, forced[1], diffusion, *couplings)
    after, before, edge, polars = exchange(
        solved, first, last, polar, north_courant, south_courant, polar_shift, 0
    )
    operands = [solved, after, before, edge, *polars]
    finals = [
        jax.ShapeDtypeStruct(costate.shape, F32),
        jax.ShapeDtypeStruct((tracers, rows, cells), F32),
    ]
    return tuple(
        pl.pallas_call(
            functools.partial(last_kernel, 0),
            grid=(1,),
            out_shape=finals,
            in_specs=[smem()]
            + [whole(x) for x in operands]
            + [step_block(x, 0) for x in couplings]
            + [whole(forced[0]), whole(surface)],
            out_specs=[whole(x) for x in finals],
            scratch_shapes=stencil_scratch,
            compiler_params=params(),
            name="last",
        )(polar_shift, *operands, *couplings, forced[0], surface)
    )


def solution(mesh):
    return jax.shard_map(
        per_device,
        mesh=mesh,
        in_specs=(
            P(None, None, "lat", "lon"),
            P(None, None, "lat", "lon"),
            P(None, "lat", "lon"),
            P(None, "lat", "lon"),
            P(None, "lat", "lon"),
            P(),
            P(None, ("lon", "lat"), None),
            P(None, ("lon", "lat")),
            P(None, ("lon", "lat")),
            P(None, None, ("lon", "lat")),
            P(None, None, ("lon", "lat")),
        ),
        out_specs=(P(None, None, "lat", "lon"), P(None, "lat", "lon")),
        check_vma=False,
    )
```

profile of v0, /device:TPU:0, one launch (start us, length us, event | category | flops | bytes accessed | tf_op | source)
XLA Modules:
  0.0 185.9 jit_solution(11894852745036826231)
XLA Ops:
  0.6 1.3 copy.13.counts
  1.9 5.3 %pack.2 = f32[2048,128]{1,0:T(8,128)} custom-call(s32[2,1]{1,0:T(2,128)} %copy.13.counts, s32[2,1,1280]{2,1,0:T(1,128)} %bitcast.13, s32[2,1280]{1,0:T(2,128)} %columns.3, f32[2,72,1280]{2,1,0:T(8,128)} %kernels.3, f32[2,8,1280]{2,1,0:T(8,128)} %misfits.3), custom_call_target="tpu_custom_call" | custom-call | tf_op jit(solution)/shard_map/pack/pallas_call | solution.py:89
  7.2 11.1 %all-to-all-start = ((f32[128,16,128]{2,1,0:T(8,128)}), f32[128,16,128]{2,1,0:T(8,128)S(1)}, u32[]{:S(2)}, u32[]{:S(2)}) async-start(f32[128,16,128]{2,1,0:T(8,128)} %bitcast.10), calls=%async_computation | async-start | bytes 2097152 | tf_op jit(solution)/shard_map/all_to_all | solution.py:523
  18.4 8.3 %first.1 = (f32[72,8,8,256]{3,2,1,0:T(8,128)}, f32[72,8,256]{2,1,0:T(8,128)}, f32[72,8,256]{2,1,0:T(8,128)}, f32[73,8,256]{2,1,0:T(8,128)}) custom-call(f32[72,8,8,256]{3,2,1,0:T(8,128)} %costate.1, f32[2,71,8,256]{3,2,1,0:T(8,128)} %diffusion.3, f32[2,8,256]{2,1,0:T(8,128)} %north.9, f32[2,8,256]{2,1,0:T(8,128)} %south.9, f32[2,8,256]{2,1,0:T(8,128)} %east.5), custom_call_target="tpu_custom_call" | custom-call | tf_op jit(solution)/shard_map/first/pallas_call | solution.py:539
  28.0 3.1 %collective-permute-start.65 = (f32[72,8,256]{2,1,0:T(8,128)}, f32[72,8,256]{2,1,0:T(8,128)S(1)}, u32[]{:S(2)}, u32[]{:S(2)}) collective-permute-start(f32[72,8,256]{2,1,0:T(8,128)} %get-tuple-element.53), channel_id=1, source_target_pairs={{0,1},{1,2},{2,3},{3,4},{4,5},{5,6},{6,7},{7,8},{8,9},{9,10},{10,1... | collective-permute-start | bytes 1769480 | tf_op jit(solution)/shard_map/ppermute | solution.py:463
  31.1 5.3 %pack.3 = f32[2048,128]{1,0:T(8,128)} custom-call(s32[2,1]{1,0:T(2,128)} %copy.13.counts, s32[2,1,1280]{2,1,0:T(1,128)} %bitcast.14, s32[2,1280]{1,0:T(2,128)} %columns.3, f32[2,72,1280]{2,1,0:T(8,128)} %kernels.3, f32[2,8,1280]{2,1,0:T(8,128)} %misfits.3), custom_call_target="tpu_custom_call" | custom-call | tf_op jit(solution)/shard_map/pack/pallas_call | solution.py:89
  37.5 11.4 %all-to-all-start.1 = ((f32[128,16,128]{2,1,0:T(8,128)}), f32[128,16,128]{2,1,0:T(8,128)S(1)}, u32[]{:S(2)}, u32[]{:S(2)}) async-start(f32[128,16,128]{2,1,0:T(8,128)} %bitcast.9), calls=%async_computation.1 | async-start | bytes 2097152 | tf_op jit(solution)/shard_map/all_to_all | solution.py:523
  49.9 4.5 %edge.2 = f32[9,8,128]{2,1,0:T(8,128)} custom-call(f32[72,8,8,256]{3,2,1,0:T(8,128)} %get-tuple-element.51.diffused, f32[72,8,256]{2,1,0:T(8,128)} %copy-done.2, f32[72,8,256]{2,1,0:T(8,128)} %copy-done.3, f32[2,8,256]{2,1,0:T(8,128)} %north.9, f32[2,8,256]{2,1,0:T(8,128)} %south.9), custom_call_target="tpu_custom_call" | custom-call | tf_op jit(solution)/shard_map/edge/pallas_call | solution.py:488
  54.5 3.8 %collective-permute-start.66 = (f32[9,8,128]{2,1,0:T(8,128)}, f32[9,8,128]{2,1,0:T(8,128)S(1)}, u32[]{:S(2)}, u32[]{:S(2)}) collective-permute-start(f32[9,8,128]{2,1,0:T(8,128)} %edge.2), channel_id=1, source_target_pairs={{0,112},{16,0},{32,16},{48,32},{64,48},{80,64},{96,80},{112,96},{1... | collective-permute-start | bytes 110600 | tf_op jit(solution)/shard_map/ppermute | solution.py:499
  62.5 3.0 %conditional.5 = (f32[73,8,256]{2,1,0:T(8,128)}, f32[73,8,256]{2,1,0:T(8,128)}) conditional(s32[]{:T(128)} %clamp.13, f32[73,8,256]{2,1,0:T(8,128)} %get-tuple-element.54, f32[73,8,256]{2,1,0:T(8,128)} %get-tuple-element.54, f32[73,8,256]{2,1,0:T(8,128)} %get-tuple-element.54, ...), branch_computations={%region_8.9_spmd, %region_9.10_spmd, %region_10.11_spmd, %region_1... | conditional | bytes 4784224 | solution.py:477
  62.5 1.5 collective-permute-start.24
  64.0 1.5 collective-permute-start.25
  65.5 16.2 %conditional.4 = (f32[73,8,256]{2,1,0:T(8,128)}, f32[73,8,256]{2,1,0:T(8,128)}) conditional(s32[]{:T(128)} %clamp.12, f32[73,8,256]{2,1,0:T(8,128)} %get-tuple-element.54, f32[73,8,256]{2,1,0:T(8,128)} %get-tuple-element.54, f32[73,8,256]{2,1,0:T(8,128)} %get-tuple-element.54, ...), branch_computations={%region_0.1_spmd, %region_1.2_spmd, %region_2.3_spmd, %region_3.4_... | conditional | bytes 4784224 | solution.py:477
  65.5 2.4 %collective-permute-start.8 = (f32[73,8,256]{2,1,0:T(8,128)}, f32[73,8,256]{2,1,0:T(8,128)}, u32[]{:S(2)}, u32[]{:S(2)}) collective-permute-start(f32[73,8,256]{2,1,0:T(8,128)} %param.4), channel_id=1, source_target_pairs={{64,0},{80,16},{96,32},{112,48},{0,64},{16,80},{32,96},{48,112}} | collective-permute-start | bytes 1794056 | tf_op jit(solution)/shard_map/cond/branch_4_fun/ppermute | solution.py:472
  67.9 2.6 %collective-permute-start.9 = (f32[73,8,256]{2,1,0:T(8,128)}, f32[73,8,256]{2,1,0:T(8,128)}, u32[]{:S(2)}, u32[]{:S(2)}) collective-permute-start(f32[73,8,256]{2,1,0:T(8,128)} %param.4), channel_id=1, source_target_pairs={{80,0},{96,16},{112,32},{0,48},{16,64},{32,80},{48,96},{64,112}} | collective-permute-start | bytes 1794056 | tf_op jit(solution)/shard_map/cond/branch_4_fun/ppermute | solution.py:472
  70.5 7.2 %collective-permute-done.8 = f32[73,8,256]{2,1,0:T(8,128)} collective-permute-done((f32[73,8,256]{2,1,0:T(8,128)}, f32[73,8,256]{2,1,0:T(8,128)}, u32[]{:S(2)}, u32[]{:S(2)}) %collective-permute-start.8) | collective-permute-done | bytes 598048 | tf_op jit(solution)/shard_map/cond/branch_4_fun/ppermute | solution.py:472
  77.7 4.1 %collective-permute-done.9 = f32[73,8,256]{2,1,0:T(8,128)} collective-permute-done((f32[73,8,256]{2,1,0:T(8,128)}, f32[73,8,256]{2,1,0:T(8,128)}, u32[]{:S(2)}, u32[]{:S(2)}) %collective-permute-start.9) | collective-permute-done | bytes 598048 | tf_op jit(solution)/shard_map/cond/branch_4_fun/ppermute | solution.py:472
  81.8 18.2 %forcing.2.forced = f32[72,8,8,256]{3,2,1,0:T(8,128)} custom-call(f32[2048,128]{1,0:T(8,128)} %bitcast.12), custom_call_target="tpu_custom_call" | custom-call | tf_op jit(solution)/shard_map/forcing/pallas_call | solution.py:148
  100.5 14.1 %middle.1 = (f32[72,8,8,256]{3,2,1,0:T(8,128)}, f32[72,8,256]{2,1,0:T(8,128)}, f32[72,8,256]{2,1,0:T(8,128)}, f32[73,8,256]{2,1,0:T(8,128)S(1)}, f32[8,8,256]{2,1,0:T(8,128)}) custom-call(s32[2,128]{1,0:T(2,128)} %shift.3, f32[72,8,8,256]{3,2,1,0:T(8,128)} %get-tuple-element.51.diffused, f32[72,8,256]{2,1,0:T(8,128)} %copy-done.2, f32[72,8,256]{2,1,0:T(8,128)} %copy-done.3, ...), custom_call_target="tpu_custom_call" | custom-call | tf_op jit(solution)/shard_map/middle/pallas_call | solution.py:554
  116.0 3.1 %collective-permute-start.68 = (f32[72,8,256]{2,1,0:T(8,128)}, f32[72,8,256]{2,1,0:T(8,128)S(1)}, u32[]{:S(2)}, u32[]{:S(2)}) collective-permute-start(f32[72,8,256]{2,1,0:T(8,128)} %get-tuple-element.61), channel_id=1, source_target_pairs={{0,1},{1,2},{2,3},{3,4},{4,5},{5,6},{6,7},{7,8},{8,9},{9,10},{10,1... | collective-permute-start | bytes 1769480 | tf_op jit(solution)/shard_map/ppermute | solution.py:463
  119.1 1.8 collective-permute-done.68.before
  121.6 4.5 %edge.3 = f32[9,8,128]{2,1,0:T(8,128)} custom-call(f32[72,8,8,256]{3,2,1,0:T(8,128)} %get-tuple-element.59.diffused, f32[72,8,256]{2,1,0:T(8,128)} %copy-done.4, f32[72,8,256]{2,1,0:T(8,128)} %copy-done.5, f32[2,8,256]{2,1,0:T(8,128)} %north.9, f32[2,8,256]{2,1,0:T(8,128)} %south.9), custom_call_target="tpu_custom_call" | custom-call | tf_op jit(solution)/shard_map/edge/pallas_call | solution.py:488
  130.9 3.0 %conditional.7 = (f32[73,8,256]{2,1,0:T(8,128)}, f32[73,8,256]{2,1,0:T(8,128)}) conditional(s32[]{:T(128)} %clamp.15, f32[73,8,256]{2,1,0:T(8,128)S(1)} %get-tuple-element.62, f32[73,8,256]{2,1,0:T(8,128)S(1)} %get-tuple-element.62, f32[73,8,256]{2,1,0:T(8,128)S(1)} %get-tuple-element.62, ...), branch_computations={%region_24.25_spmd, %region_25.26_spmd, %region_26.27_spmd, %regio... | conditional | bytes 4784224 | solution.py:477
  131.0 1.5 collective-permute-start.54
  132.5 1.5 collective-permute-start.55
  134.0 18.9 %conditional.6 = (f32[73,8,256]{2,1,0:T(8,128)}, f32[73,8,256]{2,1,0:T(8,128)}) conditional(s32[]{:T(128)} %clamp.14, f32[73,8,256]{2,1,0:T(8,128)S(1)} %get-tuple-element.62, f32[73,8,256]{2,1,0:T(8,128)S(1)} %get-tuple-element.62, f32[73,8,256]{2,1,0:T(8,128)S(1)} %get-tuple-element.62, ...), branch_computations={%region_16.17_spmd, %region_17.18_spmd, %region_18.19_spmd, %regio... | conditional | bytes 4784224 | solution.py:477
  134.0 3.4 %collective-permute-start.40 = (f32[73,8,256]{2,1,0:T(8,128)S(1)}, f32[73,8,256]{2,1,0:T(8,128)}, u32[]{:S(2)}, u32[]{:S(2)}) collective-permute-start(f32[73,8,256]{2,1,0:T(8,128)S(1)} %param.20), channel_id=1, source_target_pairs={{64,0},{80,16},{96,32},{112,48},{0,64},{16,80},{32,96},{48,112}} | collective-permute-start | bytes 1794056 | tf_op jit(solution)/shard_map/cond/branch_4_fun/ppermute | solution.py:472
  137.4 4.4 %collective-permute-start.41 = (f32[73,8,256]{2,1,0:T(8,128)S(1)}, f32[73,8,256]{2,1,0:T(8,128)}, u32[]{:S(2)}, u32[]{:S(2)}) collective-permute-start(f32[73,8,256]{2,1,0:T(8,128)S(1)} %param.20), channel_id=1, source_target_pairs={{80,0},{96,16},{112,32},{0,48},{16,64},{32,80},{48,96},{64,112}} | collective-permute-start | bytes 1794056 | tf_op jit(solution)/shard_map/cond/branch_4_fun/ppermute | solution.py:472
  141.8 4.1 %collective-permute-done.40 = f32[73,8,256]{2,1,0:T(8,128)} collective-permute-done((f32[73,8,256]{2,1,0:T(8,128)S(1)}, f32[73,8,256]{2,1,0:T(8,128)}, u32[]{:S(2)}, u32[]{:S(2)}) %collective-permute-start.40) | collective-permute-done | bytes 598048 | tf_op jit(solution)/shard_map/cond/branch_4_fun/ppermute | solution.py:472
  145.9 6.9 %collective-permute-done.41 = f32[73,8,256]{2,1,0:T(8,128)} collective-permute-done((f32[73,8,256]{2,1,0:T(8,128)S(1)}, f32[73,8,256]{2,1,0:T(8,128)}, u32[]{:S(2)}, u32[]{:S(2)}) %collective-permute-start.41) | collective-permute-done | bytes 598048 | tf_op jit(solution)/shard_map/cond/branch_4_fun/ppermute | solution.py:472
  153.8 18.2 %forcing.3.forced = f32[72,8,8,256]{3,2,1,0:T(8,128)} custom-call(f32[2048,128]{1,0:T(8,128)} %bitcast.11), custom_call_target="tpu_custom_call" | custom-call | tf_op jit(solution)/shard_map/forcing/pallas_call | solution.py:148
  172.6 13.2 %last.1 = (f32[72,8,8,256]{3,2,1,0:T(8,128)}, f32[8,8,256]{2,1,0:T(8,128)}) custom-call(s32[2,128]{1,0:T(2,128)} %shift.3, f32[72,8,8,256]{3,2,1,0:T(8,128)} %get-tuple-element.59.diffused, f32[72,8,256]{2,1,0:T(8,128)} %copy-done.4, f32[72,8,256]{2,1,0:T(8,128)} %copy-done.5, f32[9,8,128]{2,1,0:T(8,128)} %copy-done.6, ...), custom_call_target="tpu_custom_call" | custom-call | tf_op jit(solution)/shard_map/last/pallas_call | solution.py:577
  (33 shorter events, 9.3 us)
Async XLA Ops:
  7.2 30.3 %all-to-all-start = ((f32[128,16,128]{2,1,0:T(8,128)}), f32[128,16,128]{2,1,0:T(8,128)S(1)}, u32[]{:S(2)}, u32[]{:S(2)}) async-start(f32[128,16,128]{2,1,0:T(8,128)} %bitcast.10), calls=%async_computation | async-start | bytes 2097152 | tf_op jit(solution)/shard_map/all_to_all | solution.py:523
  26.7 22.2 %collective-permute-start.64 = (f32[72,8,256]{2,1,0:T(8,128)}, f32[72,8,256]{2,1,0:T(8,128)S(1)}, u32[]{:S(2)}, u32[]{:S(2)}) collective-permute-start(f32[72,8,256]{2,1,0:T(8,128)} %get-tuple-element.52), channel_id=1, source_target_pairs={{1,0},{2,1},{3,2},{4,3},{5,4},{6,5},{7,6},{8,7},{9,8},{10,9},{11,1... | collective-permute-start | bytes 1769480 | tf_op jit(solution)/shard_map/ppermute | solution.py:462
  28.0 30.3 %copy-start.8 = (s32[2,128]{1,0:T(2,128)S(1)}, s32[2,128]{1,0:T(2,128)}, u32[]{:S(2)}) copy-start(s32[2,128]{1,0:T(2,128)} %shift.3) | copy-start | bytes 3076
  28.0 20.9 %collective-permute-start.65 = (f32[72,8,256]{2,1,0:T(8,128)}, f32[72,8,256]{2,1,0:T(8,128)S(1)}, u32[]{:S(2)}, u32[]{:S(2)}) collective-permute-start(f32[72,8,256]{2,1,0:T(8,128)} %get-tuple-element.53), channel_id=1, source_target_pairs={{0,1},{1,2},{2,3},{3,4},{4,5},{5,6},{6,7},{7,8},{8,9},{9,10},{10,1... | collective-permute-start | bytes 1769480 | tf_op jit(solution)/shard_map/ppermute | solution.py:463
  37.5 44.2 %copy-start.1 = (f32[128,16,128]{2,1,0:T(8,128)}, f32[128,16,128]{2,1,0:T(8,128)S(1)}, u32[]{:S(2)}) copy-start(f32[128,16,128]{2,1,0:T(8,128)S(1)} %all-to-all-done) | copy-start | bytes 3145732
  37.5 115.3 %all-to-all-start.1 = ((f32[128,16,128]{2,1,0:T(8,128)}), f32[128,16,128]{2,1,0:T(8,128)S(1)}, u32[]{:S(2)}, u32[]{:S(2)}) async-start(f32[128,16,128]{2,1,0:T(8,128)} %bitcast.9), calls=%async_computation.1 | async-start | bytes 2097152 | tf_op jit(solution)/shard_map/all_to_all | solution.py:523
  48.9 0.8 copy-start.2
  49.0 1.0 copy-start.3
  54.5 45.5 %collective-permute-start.66 = (f32[9,8,128]{2,1,0:T(8,128)}, f32[9,8,128]{2,1,0:T(8,128)S(1)}, u32[]{:S(2)}, u32[]{:S(2)}) collective-permute-start(f32[9,8,128]{2,1,0:T(8,128)} %edge.2), channel_id=1, source_target_pairs={{0,112},{16,0},{32,16},{48,32},{64,48},{80,64},{96,80},{112,96},{1... | collective-permute-start | bytes 110600 | tf_op jit(solution)/shard_map/ppermute | solution.py:499
  62.5 3.0 %collective-permute-start.24 = (f32[73,8,256]{2,1,0:T(8,128)}, f32[73,8,256]{2,1,0:T(8,128)}, u32[]{:S(2)}, u32[]{:S(2)}) collective-permute-start(f32[73,8,256]{2,1,0:T(8,128)} %param.12), channel_id=1, source_target_pairs={{79,15},{95,31},{111,47},{127,63},{15,79},{31,95},{47,111},{63,127}} | collective-permute-start | bytes 1794056 | tf_op jit(solution)/shard_map/cond/branch_4_fun/ppermute | solution.py:472
  64.0 1.5 collective-permute-start.25
  65.5 12.2 %collective-permute-start.8 = (f32[73,8,256]{2,1,0:T(8,128)}, f32[73,8,256]{2,1,0:T(8,128)}, u32[]{:S(2)}, u32[]{:S(2)}) collective-permute-start(f32[73,8,256]{2,1,0:T(8,128)} %param.4), channel_id=1, source_target_pairs={{64,0},{80,16},{96,32},{112,48},{0,64},{16,80},{32,96},{48,112}} | collective-permute-start | bytes 1794056 | tf_op jit(solution)/shard_map/cond/branch_4_fun/ppermute | solution.py:472
  67.9 13.8 %collective-permute-start.9 = (f32[73,8,256]{2,1,0:T(8,128)}, f32[73,8,256]{2,1,0:T(8,128)}, u32[]{:S(2)}, u32[]{:S(2)}) collective-permute-start(f32[73,8,256]{2,1,0:T(8,128)} %param.4), channel_id=1, source_target_pairs={{80,0},{96,16},{112,32},{0,48},{16,64},{32,80},{48,96},{64,112}} | collective-permute-start | bytes 1794056 | tf_op jit(solution)/shard_map/cond/branch_4_fun/ppermute | solution.py:472
  99.9 0.6 copy-start.7
  114.7 4.4 %collective-permute-start.67 = (f32[72,8,256]{2,1,0:T(8,128)}, f32[72,8,256]{2,1,0:T(8,128)S(1)}, u32[]{:S(2)}, u32[]{:S(2)}) collective-permute-start(f32[72,8,256]{2,1,0:T(8,128)} %get-tuple-element.60), channel_id=1, source_target_pairs={{1,0},{2,1},{3,2},{4,3},{5,4},{6,5},{7,6},{8,7},{9,8},{10,9},{11,1... | collective-permute-start | bytes 1769480 | tf_op jit(solution)/shard_map/ppermute | solution.py:462
  116.0 4.9 %collective-permute-start.68 = (f32[72,8,256]{2,1,0:T(8,128)}, f32[72,8,256]{2,1,0:T(8,128)S(1)}, u32[]{:S(2)}, u32[]{:S(2)}) collective-permute-start(f32[72,8,256]{2,1,0:T(8,128)} %get-tuple-element.61), channel_id=1, source_target_pairs={{0,1},{1,2},{2,3},{3,4},{4,5},{5,6},{6,7},{7,8},{8,9},{9,10},{10,1... | collective-permute-start | bytes 1769480 | tf_op jit(solution)/shard_map/ppermute | solution.py:463
  119.0 1.8 copy-start.4
  120.8 0.8 copy-start.5
  126.2 45.8 %collective-permute-start.69 = (f32[9,8,128]{2,1,0:T(8,128)}, f32[9,8,128]{2,1,0:T(8,128)S(1)}, u32[]{:S(2)}, u32[]{:S(2)}) collective-permute-start(f32[9,8,128]{2,1,0:T(8,128)} %edge.3), channel_id=1, source_target_pairs={{0,112},{16,0},{32,16},{48,32},{64,48},{80,64},{96,80},{112,96},{1... | collective-permute-start | bytes 110600 | tf_op jit(solution)/shard_map/ppermute | solution.py:499
  131.0 3.0 %collective-permute-start.54 = (f32[73,8,256]{2,1,0:T(8,128)S(1)}, f32[73,8,256]{2,1,0:T(8,128)}, u32[]{:S(2)}, u32[]{:S(2)}) collective-permute-start(f32[73,8,256]{2,1,0:T(8,128)S(1)} %param.27), channel_id=1, source_target_pairs={{63,15},{79,31},{95,47},{111,63},{127,79},{15,95},{31,111},{47,127}} | collective-permute-start | bytes 1794056 | tf_op jit(solution)/shard_map/cond/branch_3_fun/ppermute | solution.py:472
  132.5 1.5 collective-permute-start.55
  134.0 12.0 %collective-permute-start.40 = (f32[73,8,256]{2,1,0:T(8,128)S(1)}, f32[73,8,256]{2,1,0:T(8,128)}, u32[]{:S(2)}, u32[]{:S(2)}) collective-permute-start(f32[73,8,256]{2,1,0:T(8,128)S(1)} %param.20), channel_id=1, source_target_pairs={{64,0},{80,16},{96,32},{112,48},{0,64},{16,80},{32,96},{48,112}} | collective-permute-start | bytes 1794056 | tf_op jit(solution)/shard_map/cond/branch_4_fun/ppermute | solution.py:472
  137.4 15.5 %collective-permute-start.41 = (f32[73,8,256]{2,1,0:T(8,128)S(1)}, f32[73,8,256]{2,1,0:T(8,128)}, u32[]{:S(2)}, u32[]{:S(2)}) collective-permute-start(f32[73,8,256]{2,1,0:T(8,128)S(1)} %param.20), channel_id=1, source_target_pairs={{80,0},{96,16},{112,32},{0,48},{16,64},{32,80},{48,96},{64,112}} | collective-permute-start | bytes 1794056 | tf_op jit(solution)/shard_map/cond/branch_4_fun/ppermute | solution.py:472
  152.9 1.0 copy-start
  172.0 0.6 copy-start.6
where the time goes:
time: 188 us; the launch traced here: 186 us
  Pallas kernels  91.7 us (49%)
  starting transfers between devices  54.8 us (29%)
  waiting for transfers between devices  25.2 us (13%)
  between operations  8.14 us (4%)
  local copies, waits for them, and re-layouts  5.93 us (3%)
    pallas_call x2, Pallas kernels, forcing(): pl.pallas_call(forcing_kernel, out_shape=jax.ShapeDtypeStruct((levels, ro...  36.3 us
    all_to_all x2, starting transfers between devices, exchanged(): lax.all_to_all(sent, AXES, 0, 0, tiled=True).reshape(devices * CAP, LANES)  22.5 us
    ppermute x8, waiting for transfers between devices, route(): return lax.ppermute(row, AXES, pairs)  22.3 us
    ppermute x8, starting transfers between devices, route(): return lax.ppermute(row, AXES, pairs)  18.8 us
    pallas_call x1, Pallas kernels, per_device(): pl.pallas_call(functools.partial(middle_kernel, 1), grid=(1,), out_shape=...  14.1 us
    pallas_call x1, Pallas kernels, per_device(): pl.pallas_call(functools.partial(last_kernel, 0), grid=(1,), out_shape=fi...  13.2 us
    pallas_call x2, Pallas kernels, packed(): pl.pallas_call(functools.partial(pack_kernel, step), grid=(1,), out_shape...  10.6 us
    pallas_call x2, Pallas kernels, exchange(): pl.pallas_call(edge_kernel, grid=(1,), out_shape=jax.ShapeDtypeStruct((le...  9.04 us
  transfers between devices with their start and end apart: 16, of which 6 were waited for; matrix products, arithmetic and copies ran while one was open for 0% of the time, Pallas kernels for 39%

commit v1 on v0

v1 whole, which is shorter than its diff:
```python
import functools

import jax
import jax.numpy as jnp
from jax import lax
from jax.experimental import pallas as pl
from jax.experimental.pallas import tpu as pltpu
from jax.sharding import PartitionSpec as P

AXES = ("lon", "lat")
LANES = 128
CAP = 16
GROUP = 8
F32 = jnp.float32
BF16 = jnp.bfloat16
VMEM_LIMIT = 56 * 1024 * 1024


def vmem():
    return pl.BlockSpec(memory_space=pltpu.VMEM)


def smem():
    return pl.BlockSpec(memory_space=pltpu.SMEM)


def params():
    return pltpu.CompilerParams(vmem_limit_bytes=VMEM_LIMIT)


def dot(a, b, contract=((1,), (0,))):
    return lax.dot_general(a, b, (contract, ((), ())), preferred_element_type=F32)


def halves(x):
    high = x.astype(BF16)
    return high, (x - high.astype(F32)).astype(BF16)


def pack_kernel(counts, owners, columns, kernels, misfits, out, payload, target):
    steps, levels, held = kernels.shape
    tracers = misfits.shape[1]
    shape = (LANES, LANES)
    device = lax.broadcasted_iota(jnp.int32, shape, 0)
    table = counting_table()
    for step in range(steps):
        owner = owners[step]
        live = lax.broadcasted_iota(jnp.int32, owner.shape, 1) < counts[step, 0]
        owner = jnp.where(live, owner, -1)
        seen = jnp.zeros(shape, F32)
        for start in range(0, held, LANES):
            here = owner[:, start : start + LANES]
            hot = device == here
            counted = dot(jnp.where(hot, 1.0, 0.0).astype(BF16), table)
            rank = jnp.sum(
                jnp.where(hot, counted[:, :LANES] + seen, 0.0), axis=0, keepdims=True
            )
            seen = seen + counted[:, LANES:]
            target[:, start : start + LANES] = jnp.where(
                here >= 0, here * CAP + rank.astype(jnp.int32), -1
            )
        column = columns[step : step + 1, :].astype(F32) + 1.0
        column = jnp.where(lax.broadcasted_iota(jnp.int32, (8, held), 0) == 0, column, 0.0)
        unused = jnp.zeros((LANES - levels - tracers - 8, held), F32)
        high, low = halves(
            jnp.concatenate([kernels[step], misfits[step], column, unused], axis=0)
        )
        payload[:LANES, :] = high
        payload[LANES:, :] = low
        owned = 256 // CAP

        def place(i, carry):
            slot = lax.broadcasted_iota(jnp.int32, (owned * CAP, held), 0) + i * owned * CAP
            hot = jnp.where(slot == target[...], 1.0, 0.0).astype(BF16)
            both = dot(hot, payload[...], ((1,), (1,)))
            both = both[:, :LANES] + both[:, LANES:]
            out[pl.ds(i * owned, owned), step * CAP : (step + 1) * CAP, :] = both.reshape(
                owned, CAP, LANES
            )
            return carry

        lax.fori_loop(0, out.shape[0] // owned, place, 0)


def counting_table():
    shape = (LANES, LANES)
    earlier = lax.broadcasted_iota(jnp.int32, shape, 0) < lax.broadcasted_iota(
        jnp.int32, shape, 1
    )
    return jnp.concatenate(
        [jnp.where(earlier, 1.0, 0.0), jnp.ones(shape, F32)], axis=1
    ).astype(BF16)


def packed(counts, owners, columns, kernels, misfits):
    steps, held = columns.shape
    devices = lax.axis_size("lon") * lax.axis_size("lat")
    return pl.pallas_call(
        pack_kernel,
        out_shape=jax.ShapeDtypeStruct((devices, steps * CAP, LANES), F32),
        in_specs=[smem()] + [vmem()] * 4,
        out_specs=vmem(),
        scratch_shapes=[
            pltpu.VMEM((2 * LANES, held), BF16),
            pltpu.VMEM((1, held), jnp.int32),
        ],
        compiler_params=params(),
        name="pack",
    )(counts, owners, columns, kernels, misfits)


def forcing_kernel(step, received, out, fields, hots, place, ordered):
    levels, rows, tracers, cells = out.shape
    slots = received.shape[0] * CAP
    blocks = slots // LANES
    sources = LANES // CAP
    sub = lax.broadcasted_iota(jnp.int32, (rows, LANES), 0)
    at_column = levels + tracers
    for b in range(blocks):
        span = slice(b * LANES, (b + 1) * LANES)
        block = received[b * sources : (b + 1) * sources, step * CAP : (step + 1) * CAP, :]
        turned = block.reshape(LANES, LANES).T
        high, low = halves(turned)
        fields[:LANES, span] = high
        fields[LANES:, span] = low
        row = (turned[at_column : at_column + 1].astype(jnp.int32) - 1) >> 8
        hots[b * rows : (b + 1) * rows, :] = jnp.where(sub == row, 1.0, 0.0)
    counted = dot(hots[...].astype(BF16), counting_table())
    run = jnp.zeros((rows, LANES), F32)
    runs = []
    for b in range(blocks):
        runs.append(run)
        run = run + counted[b * rows : (b + 1) * rows, LANES:]
    filled = jnp.floor((run + (LANES - 1.0)) * (1.0 / LANES))
    start = jnp.zeros((rows, LANES), F32)
    for j in range(1, rows):
        start = start + jnp.where(sub >= j, pltpu.roll(filled, j, 0), 0.0)
    for b in range(blocks):
        hot = hots[b * rows : (b + 1) * rows, :]
        at = counted[b * rows : (b + 1) * rows, :LANES] + runs[b] + start * float(LANES)
        at = jnp.sum(hot * at, axis=0, keepdims=True)
        live = jnp.sum(hot, axis=0, keepdims=True) > 0.0
        place[:, b * LANES : (b + 1) * LANES] = jnp.where(live, at, -1.0)
    counts = [jnp.max(filled[r : r + 1, :]).astype(jnp.int32) for r in range(rows)]
    used = sum(counts)
    wide = 2 * LANES

    def sort(i, carry):
        slot = (lax.broadcasted_iota(jnp.int32, (wide, slots), 0) + i * wide).astype(F32)
        hot = jnp.where(slot == place[...], 1.0, 0.0).astype(BF16)
        both = dot(fields[...], hot, ((1,), (1,)))
        ordered[:, pl.ds(pl.multiple_of(i * wide, wide), wide)] = both[:LANES] + both[LANES:]
        return carry

    lax.fori_loop(0, (used + 1) // 2, sort, 0)
    out[...] = jnp.zeros_like(out)
    cell = lax.broadcasted_iota(jnp.int32, (cells, LANES), 0)
    first = jnp.int32(0)
    for r in range(rows):
        names = (cell + (r * cells + 1)).astype(F32)

        def add(p, carry):
            block = ordered[:, pl.ds(pl.multiple_of(p * LANES, LANES), LANES)]
            hot = jnp.where(names == block[at_column : at_column + 1], 1.0, 0.0).astype(BF16)
            product = block[:levels][:, None, :] * block[levels:at_column][None]
            high, low = halves(product.reshape(levels * tracers, LANES))
            total = dot(high, hot, ((1,), (1,))) + dot(low, hot, ((1,), (1,)))
            out[:, r, :, :] += total.reshape(levels, tracers, cells)
            return carry

        lax.fori_loop(first, first + counts[r], add, 0)
        first = first + counts[r]


def forcing(step, received, levels, tracers, rows, cells):
    slots = received.shape[0] * CAP
    return pl.pallas_call(
        functools.partial(forcing_kernel, step),
        out_shape=jax.ShapeDtypeStruct((levels, rows, tracers, cells), F32),
        in_specs=[vmem()],
        out_specs=vmem(),
        scratch_shapes=[
            pltpu.VMEM((2 * LANES, slots), BF16),
            pltpu.VMEM((slots // LANES * rows, LANES), F32),
            pltpu.VMEM((1, slots), F32),
            pltpu.VMEM((LANES, slots + rows * LANES), F32),
        ],
        compiler_params=params(),
        name="forcing",
    )(received)


def spread(x, row, tracers):
    return jnp.broadcast_to(x[row : row + 1, :], (tracers, x.shape[1]))


def eliminate(level, above, carry, rights, ratios):
    below, ratio, values = carry
    if above is None:
        above = jnp.zeros_like(below)
    inverse = 1.0 / (1.0 + below + above + below * ratio)
    lower = below * inverse
    ratio = -above * inverse
    ratios[level] = ratio
    tracers = rights[0].shape[0]
    fresh = [
        spread(inverse, r, tracers) * rights[r] + spread(lower, r, tracers) * values[r]
        for r in range(len(rights))
    ]
    return (above, ratio, fresh)


def substitute(diffused, ratios, north, south, east, first, last, polar, column):
    levels, rows, tracers, cells = diffused.shape
    lat = lax.axis_index("lat")
    at_start = lat == 0
    picked_north = jnp.where(at_start, north[0, 0:1, :], north[0, rows - 1 : rows, :])
    picked_south = jnp.where(at_start, south[0, 0:1, :], south[0, rows - 1 : rows, :])
    own = jnp.broadcast_to(1.0 - picked_north - picked_south, (tracers, cells))
    side = jnp.broadcast_to(jnp.where(at_start, picked_north, picked_south), (tracers, cells))
    picked_east = jnp.where(at_start, east[0, 0:1, :], east[0, rows - 1 : rows, :])
    groups = levels // GROUP
    polar[:, groups, 0, :] = jnp.broadcast_to(picked_east, (tracers, cells))
    lane = lax.broadcasted_iota(jnp.int32, (tracers, LANES), 1)

    def group(i, solved):
        at = groups - 1 - i
        west = jnp.zeros((tracers, LANES), F32)
        for j in range(GROUP - 1, -1, -1):
            level = at * GROUP + j
            ratio = ratios[level]
            fresh = []
            for r in range(rows):
                value = diffused[level, r] - spread(ratio, r, tracers) * solved[r]
                diffused[level, r] = value
                fresh.append(value)
                lanes = j * rows + r
                moved = pltpu.roll(value[:, :LANES], lanes, 1) if lanes else value[:, :LANES]
                west = jnp.where(lane == lanes, moved, west)
            solved = fresh
            first[level] = solved[0]
            last[level] = solved[rows - 1]
            polar[:, at, j, :] = own * jnp.where(
                at_start, solved[0], solved[rows - 1]
            ) + side * jnp.where(at_start, solved[1], solved[rows - 2])
        column[at] = west
        return solved

    lax.fori_loop(0, groups, group, [jnp.zeros((tracers, cells), F32)] * rows)


def first_kernel(
    costate, diffusion, north, south, east, diffused, first, last, polar, column, ratios
):
    levels, tracers, rows, cells = costate.shape
    zero = jnp.zeros((rows, cells), F32)
    carry = (zero, zero, [jnp.zeros((tracers, cells), F32)] * rows)

    def forward(level, above, carry):
        rights = [costate[level, :, r, :] for r in range(rows)]
        carry = eliminate(level, above, carry, rights, ratios)
        for r in range(rows):
            diffused[level, r] = carry[2][r]
        return carry

    def group(i, carry):
        for j in range(GROUP):
            level = i * GROUP + j
            carry = forward(level, diffusion[0, level], carry)
        return carry

    carry = lax.fori_loop(0, levels // GROUP - 1, group, carry)
    for level in range(levels - GROUP, levels):
        carry = forward(level, diffusion[0, level] if level < levels - 1 else None, carry)
    substitute(diffused, ratios, north, south, east, first, last, polar, column)


def meridional(level, row, diffused, after, before, coefs):
    rows = diffused.shape[1]
    own, north, south = coefs
    up = diffused[level, row + 1] if row < rows - 1 else after[level]
    down = diffused[level, row - 1] if row > 0 else before[level]
    return own * diffused[level, row] + north * up + south * down


def edge_kernel(column, after, before, north, south, edge):
    groups, tracers, lanes = column.shape
    rows = north.shape[1]
    lane = lax.broadcasted_iota(jnp.int32, (tracers, lanes), 1)

    def along_lanes(x):
        shape = (rows, lanes)
        own_lane = (lax.broadcasted_iota(jnp.int32, shape, 1) & (rows - 1)) == (
            lax.broadcasted_iota(jnp.int32, shape, 0)
        )
        picked = jnp.where(own_lane, jnp.broadcast_to(x[0, :, :1], shape), 0.0)
        return jnp.broadcast_to(jnp.sum(picked, axis=0, keepdims=True), (tracers, lanes))

    n, s = along_lanes(north), along_lanes(south)
    own = 1.0 - n - s

    def group(i, carry):
        here = column[i]
        up = pltpu.roll(here, lanes - 1, 1)
        down = pltpu.roll(here, 1, 1)
        for j in range(GROUP):
            level = i * GROUP + j
            bottom, top = j * rows, j * rows + rows - 1
            up = jnp.where(lane == top, pltpu.roll(after[level], top, 1), up)
            moved = pltpu.roll(before[level], bottom, 1) if bottom else before[level]
            down = jnp.where(lane == bottom, moved, down)
        edge[i] = own * here + n * up + s * down
        return carry

    lax.fori_loop(0, groups, group, 0)


def rotate_kernel(step, shift, circle, out, moved):
    parts, groups, group, cells = out.shape
    lat = lax.axis_index("lat")
    last_lat = lax.axis_size("lat") - 1
    rows = shift.shape[1] // lax.axis_size("lat")

    @pl.when((lat == 0) | (lat == last_lat))
    def _():
        amount = jnp.where(lat == 0, shift[step, 0], shift[step, rows * last_lat + rows - 1])
        amount = lax.rem(amount + 2 * parts * cells, parts * cells)
        hops = amount // cells
        inner = amount - hops * cells
        shape = (group, cells)
        lane = lax.broadcasted_iota(jnp.int32, shape, 1)
        back = lax.rem(cells - inner, cells)
        for part in range(parts):
            weight = jnp.broadcast_to(circle[part, groups, 0:1, :], shape)
            for g in range(groups):
                here = circle[part, g]
                following = jnp.where(
                    lane == cells - 1,
                    pltpu.roll(circle[(part + 1) % parts, g], cells - 1, 1),
                    pltpu.roll(here, cells - 1, 1),
                )
                moved[part, g] = pltpu.roll(here + weight * (following - here), back, 1)
        for part in range(parts):
            low = lax.rem(part + hops, parts)
            high = lax.rem(part + hops + 1, parts)
            for g in range(groups):
                out[part, g] = jnp.where(lane < cells - inner, moved[low, g], moved[high, g])


def prepare_stencil(north, south, east, coefs):
    rows, cells = north.shape[1:]
    tracers = coefs.shape[2]
    for r in range(rows):
        n = north[0, r : r + 1, :]
        s = south[0, r : r + 1, :]
        coefs[0, r] = jnp.broadcast_to(1.0 - n - s, (tracers, cells))
        coefs[1, r] = jnp.broadcast_to(n, (tracers, cells))
        coefs[2, r] = jnp.broadcast_to(s, (tracers, cells))
        coefs[3, r] = jnp.broadcast_to(east[0, r : r + 1, :], (tracers, cells))


def transported(group, lane_at, diffused, after, before, edge_row, coefs, turned):
    level = group * GROUP + lane_at
    rows, tracers, cells = diffused.shape[1:]
    lat = lax.axis_index("lat")
    last = lax.broadcasted_iota(jnp.int32, (tracers, cells), 1) == cells - 1
    result = []
    for r in range(rows):
        mer = meridional(level, r, diffused, after, before, [coefs[k, r] for k in range(3)])
        arrived = pltpu.roll(edge_row, LANES - 1 - (lane_at * rows + r), 1)
        arrived = jnp.concatenate([arrived] * (cells // LANES), axis=1)
        following = jnp.where(last, arrived, pltpu.roll(mer, cells - 1, 1))
        result.append(mer + coefs[3, r] * (following - mer))
    polar = turned[:, group, lane_at, :]
    result[0] = jnp.where(lat == 0, polar, result[0])
    result[rows - 1] = jnp.where(lat == lax.axis_size("lat") - 1, polar, result[rows - 1])
    return result


def middle_kernel(
    diffused,
    after,
    before,
    edge,
    turned,
    north,
    south,
    east,
    forced,
    diffusion,
    next_north,
    next_south,
    next_east,
    solved,
    first,
    last,
    polar,
    column,
    surface,
    coefs,
    ratios,
):
    levels, rows, tracers, cells = diffused.shape
    prepare_stencil(north, south, east, coefs)
    zero = jnp.zeros((rows, cells), F32)
    carry = (zero, zero, [jnp.zeros((tracers, cells), F32)] * rows)

    def forward(g, j, above, edge_row, carry):
        level = g * GROUP + j
        rights = transported(g, j, diffused, after, before, edge_row, coefs, turned)
        rights = [rights[r] + forced[level, r] for r in range(rows)]
        if above is None:
            for r in range(rows):
                surface[r] = rights[r]
        carry = eliminate(level, above, carry, rights, ratios)
        for r in range(rows):
            solved[level, r] = carry[2][r]
        return carry

    def group(i, carry):
        edge_row = edge[i]
        for j in range(GROUP):
            carry = forward(i, j, diffusion[0, i * GROUP + j], edge_row, carry)
        return carry

    groups = levels // GROUP
    carry = lax.fori_loop(0, groups - 1, group, carry)
    edge_row = edge[groups - 1]
    for j in range(GROUP):
        level = levels - GROUP + j
        above = diffusion[0, level] if level < levels - 1 else None
        carry = forward(groups - 1, j, above, edge_row, carry)
    substitute(
        solved, ratios, next_north, next_south, next_east, first, last, polar, column
    )


def last_kernel(
    diffused,
    after,
    before,
    edge,
    turned,
    north,
    south,
    east,
    forced,
    surface,
    state,
    gradient,
    coefs,
):
    levels, rows, tracers, cells = diffused.shape
    prepare_stencil(north, south, east, coefs)

    def group(i, carry):
        edge_row = edge[i]
        for j in range(GROUP):
            level = i * GROUP + j
            values = transported(i, j, diffused, after, before, edge_row, coefs, turned)
            for r in range(rows):
                state[level, :, r, :] = values[r] + forced[level, r]
        return carry

    lax.fori_loop(0, levels // GROUP, group, 0)
    for r in range(rows):
        gradient[:, r, :] = surface[r] + state[levels - 1, :, r, :]


def step_block(array, step):
    shape = (1,) + array.shape[1:]
    return pl.BlockSpec(shape, lambda i: (step,) + (0,) * (len(shape) - 1))


def whole(array):
    return pl.BlockSpec(array.shape, lambda i: (0,) * len(array.shape))


def exchange(first, last, polar, column, north, south, shift, step):
    lat_count = lax.axis_size("lat")
    lon_count = lax.axis_size("lon")
    up = [(i, i + 1) for i in range(lat_count - 1)]
    down = [(j, i) for i, j in up]
    circle = lax.all_to_all(polar, "lon", 0, 0, tiled=True)
    after = lax.ppermute(first, "lat", down)
    before = lax.ppermute(last, "lat", up)
    parts, groups, group, cells = polar.shape
    turned = pl.pallas_call(
        functools.partial(rotate_kernel, step),
        out_shape=jax.ShapeDtypeStruct((parts, groups - 1, group, cells), F32),
        in_specs=[smem(), vmem()],
        out_specs=vmem(),
        scratch_shapes=[pltpu.VMEM((parts, groups - 1, group, cells), F32)],
        compiler_params=params(),
        name="rotate",
    )(shift, circle)
    turned = lax.all_to_all(turned, "lon", 0, 0, tiled=True)
    tile = pl.BlockSpec(after.shape[:2] + (LANES,), lambda i: (0, 0, 0))
    edge = pl.pallas_call(
        edge_kernel,
        grid=(1,),
        out_shape=jax.ShapeDtypeStruct(column.shape, F32),
        in_specs=[whole(column), tile, tile] + [step_block(north, step)] * 2,
        out_specs=whole(column),
        compiler_params=params(),
        name="edge",
    )(column, after, before, north, south)
    west = [(i, (i - 1) % lon_count) for i in range(lon_count)]
    return after, before, lax.ppermute(edge, "lon", west), turned


def per_device(
    costate,
    diffusion,
    east_courant,
    north_courant,
    south_courant,
    polar_shift,
    owners,
    columns,
    sounding_counts,
    kernels,
    misfits,
):
    levels, tracers, rows, cells = costate.shape
    devices = lax.axis_size("lon") * lax.axis_size("lat")
    owner_rows = owners.reshape(owners.shape[0], 1, owners.shape[1])
    couplings = [north_courant, south_courant, east_courant]

    sent = packed(sounding_counts, owner_rows, columns, kernels, misfits)
    got = lax.all_to_all(sent, AXES, 0, 0, tiled=True)
    forced = {step: forcing(step, got, levels, tracers, rows, cells) for step in (1, 0)}

    solved_shapes = [
        jax.ShapeDtypeStruct((levels, rows, tracers, cells), F32),
        jax.ShapeDtypeStruct((levels, tracers, cells), F32),
        jax.ShapeDtypeStruct((levels, tracers, cells), F32),
        jax.ShapeDtypeStruct((tracers, levels // GROUP + 1, GROUP, cells), F32),
        jax.ShapeDtypeStruct((levels // GROUP, tracers, LANES), F32),
    ]
    ratio_scratch = pltpu.VMEM((levels, rows, cells), F32)
    stencil_scratch = [pltpu.VMEM((4, rows, tracers, cells), F32)]
    diffused, *boundary = pl.pallas_call(
        first_kernel,
        grid=(1,),
        out_shape=solved_shapes,
        in_specs=[whole(costate)] + [step_block(x, 1) for x in [diffusion] + couplings],
        out_specs=[whole(x) for x in solved_shapes],
        scratch_shapes=[ratio_scratch],
        compiler_params=params(),
        name="first",
    )(costate, diffusion, *couplings)
    incoming = exchange(*boundary, north_courant, south_courant, polar_shift, 1)
    surface_shape = jax.ShapeDtypeStruct((rows, tracers, cells), F32)
    operands = [diffused, *incoming]
    solved, *boundary, surface = pl.pallas_call(
        middle_kernel,
        grid=(1,),
        out_shape=solved_shapes + [surface_shape],
        in_specs=[whole(x) for x in operands]
        + [step_block(x, 1) for x in couplings]
        + [whole(forced[1])]
        + [step_block(x, 0) for x in [diffusion] + couplings],
        out_specs=[whole(x) for x in solved_shapes + [surface_shape]],
        scratch_shapes=stencil_scratch + [ratio_scratch],
        compiler_params=params(),
        name="middle",
    )(*operands, *couplings, forced[1], diffusion, *couplings)
    incoming = exchange(*boundary, north_courant, south_courant, polar_shift, 0)
    operands = [solved, *incoming]
    finals = [
        jax.ShapeDtypeStruct(costate.shape, F32),
        jax.ShapeDtypeStruct((tracers, rows, cells), F32),
    ]
    return tuple(
        pl.pallas_call(
            last_kernel,
            grid=(1,),
            out_shape=finals,
            in_specs=[whole(x) for x in operands]
            + [step_block(x, 0) for x in couplings]
            + [whole(forced[0]), whole(surface)],
            out_specs=[whole(x) for x in finals],
            scratch_shapes=stencil_scratch,
            compiler_params=params(),
            name="last",
        )(*operands, *couplings, forced[0], surface)
    )


def solution(mesh):
    return jax.shard_map(
        per_device,
        mesh=mesh,
        in_specs=(
            P(None, None, "lat", "lon"),
            P(None, None, "lat", "lon"),
            P(None, "lat", "lon"),
            P(None, "lat", "lon"),
            P(None, "lat", "lon"),
            P(),
            P(None, ("lon", "lat"), None),
            P(None, ("lon", "lat")),
            P(None, ("lon", "lat")),
            P(None, None, ("lon", "lat")),
            P(None, None, ("lon", "lat")),
        ),
        out_specs=(P(None, None, "lat", "lon"), P(None, "lat", "lon")),
        check_vma=False,
    )
```

time: 188 us -> 163 us (0.87)
  starting transfers between devices: 54.8 us -> 44.2 us
  between operations: 8.14 us -> 0.79 us
  Pallas kernels: 91.7 us -> 85.1 us
    all_to_all x2 -> x5, waiting for transfers between devices: 1.11 us -> 25.9 us  [the longest x1 19.8 us: per_device(): got = lax.all_to_all(sent, AXES, 0, 0, tiled=True)]
    ppermute x10 -> x2, waiting for transfers between devices: 22.3 us -> 0.01 us  [exchange(): return (after, before, lax.ppermute(edge, 'lon', west), turned)]
    ppermute x10 -> x2, starting transfers between devices: 23.6 us -> 8.13 us  [exchange(): return (after, before, lax.ppermute(edge, 'lon', west), turned)]
    pallas_call x8 -> x9, Pallas kernels: 83.4 us -> 76 us  [the longest x2 27.8 us: forcing(): pl.pallas_call(functools.partial(forcing_kernel, step), out_shape=jax.Sha...]
    all_to_all x2 -> x5, starting transfers between devices: 22.5 us -> 26.5 us  [the longest x2 9.95 us: exchange(): circle = lax.all_to_all(polar, 'lon', 0, 0, tiled=True)]
    unnamed x19 -> x23, local copies, waits for them, and re-layouts: 5.31 us -> 4.97 us
  transfers between devices with their start and end apart: 16 -> 11, of which waited for: 6 -> 3; matrix products, arithmetic and copies ran while one was open for 0% -> 0% of each run, Pallas kernels for 39% -> 34%
where the time goes in v1:
time: 163 us; the launch traced here: 161 us
  Pallas kernels  85.1 us (52%)
  starting transfers between devices  44.2 us (27%)
  waiting for transfers between devices  25.9 us (16%)
  local copies, waits for them, and re-layouts  4.97 us (3%)
    pallas_call x2, Pallas kernels, forcing(): pl.pallas_call(functools.partial(forcing_kernel, step), out_shape=jax.Sha...  27.8 us
    all_to_all x1, waiting for transfers between devices, per_device(): got = lax.all_to_all(sent, AXES, 0, 0, tiled=True)  19.8 us
    pallas_call x1, Pallas kernels, per_device(): pl.pallas_call(middle_kernel, grid=(1,), out_shape=solved_shapes + [surfa...  11.9 us
    pallas_call x2, Pallas kernels, exchange(): pl.pallas_call(functools.partial(rotate_kernel, step), out_shape=jax.Shap...  11.7 us
    pallas_call x1, Pallas kernels, per_device(): pl.pallas_call(last_kernel, grid=(1,), out_shape=finals, in_specs=[whole(...  10.2 us
    all_to_all x2, starting transfers between devices, exchange(): circle = lax.all_to_all(polar, 'lon', 0, 0, tiled=True)  9.95 us
    all_to_all x1, starting transfers between devices, per_device(): got = lax.all_to_all(sent, AXES, 0, 0, tiled=True)  9.49 us
    pallas_call x1, Pallas kernels, packed(): pl.pallas_call(pack_kernel, out_shape=jax.ShapeDtypeStruct((devices, step...  9.22 us
  transfers between devices with their start and end apart: 11, of which 3 were waited for; matrix products, arithmetic and copies ran while one was open for 0% of the time, Pallas kernels for 34%

profile of v1, /device:TPU:0, one launch (start us, length us, event | category | flops | bytes accessed | tf_op | source)
XLA Modules:
  0.0 160.9 jit_solution(12330400329637173939)
XLA Ops:
  0.6 9.0 %first.1 = (f32[72,8,8,256]{3,2,1,0:T(8,128)}, f32[72,8,256]{2,1,0:T(8,128)}, f32[72,8,256]{2,1,0:T(8,128)}, f32[8,10,8,256]{3,2,1,0:T(8,128)}, f32[9,8,128]{2,1,0:T(8,128)}) custom-call(f32[72,8,8,256]{3,2,1,0:T(8,128)} %costate.1, f32[2,71,8,256]{3,2,1,0:T(8,128)} %diffusion.3, f32[2,8,256]{2,1,0:T(8,128)} %north.9, f32[2,8,256]{2,1,0:T(8,128)} %south.9, ...), custom_call_target="tpu_custom_call" | custom-call | tf_op jit(solution)/shard_map/first/pallas_call | solution.py:543
  9.7 6.4 %all-to-all-start = ((f32[8,10,8,256]{3,2,1,0:T(8,128)}), f32[8,10,8,256]{3,2,1,0:T(8,128)S(1)}, u32[]{:S(2)}, u32[]{:S(2)}) async-start(f32[8,10,8,256]{3,2,1,0:T(8,128)} %get-tuple-element.17), calls=%async_computation | async-start | bytes 1310720 | tf_op jit(solution)/shard_map/all_to_all | solution.py:484
  16.1 0.6 copy.13.counts
  16.7 9.2 %pack.1 = f32[128,32,128]{2,1,0:T(8,128)} custom-call(s32[2,1]{1,0:T(2,128)} %copy.13.counts, s32[2,1,1280]{2,1,0:T(1,128)} %bitcast.1, s32[2,1280]{1,0:T(2,128)} %columns.1, f32[2,72,1280]{2,1,0:T(8,128)} %kernels.1, f32[2,8,1280]{2,1,0:T(8,128)} %misfits.1), custom_call_target="tpu_custom_call" | custom-call | tf_op jit(solution)/shard_map/pack/pallas_call | solution.py:98
  25.9 0.8 all-to-all-done.circle
  26.7 9.5 %all-to-all-start.2 = ((f32[128,32,128]{2,1,0:T(8,128)}), f32[128,32,128]{2,1,0:T(8,128)S(1)}, u32[]{:S(2)}, u32[]{:S(2)}) async-start(f32[128,32,128]{2,1,0:T(8,128)} %pack.1), calls=%async_computation.2 | async-start | bytes 4194304 | tf_op jit(solution)/shard_map/all_to_all | solution.py:531
  36.2 1.3 collective-permute-start
  37.5 3.9 %collective-permute-start.1 = (f32[72,8,256]{2,1,0:T(8,128)}, f32[72,8,256]{2,1,0:T(8,128)}, u32[]{:S(2)}, u32[]{:S(2)}) collective-permute-start(f32[72,8,256]{2,1,0:T(8,128)} %get-tuple-element.15), channel_id=1, source_target_pairs={{0,1},{1,2},{2,3},{3,4},{4,5},{5,6},{6,7},{7,8},{8,9},{9,10},{10,1... | collective-permute-start | bytes 1769480 | tf_op jit(solution)/shard_map/ppermute | solution.py:486
  41.4 5.8 %rotate.2 = f32[8,9,8,256]{3,2,1,0:T(8,128)} custom-call(s32[2,128]{1,0:T(2,128)} %shift.3, f32[8,10,8,256]{3,2,1,0:T(8,128)} %copy-done.1), custom_call_target="tpu_custom_call" | custom-call | tf_op jit(solution)/shard_map/rotate/pallas_call | solution.py:488
  47.3 19.8 %all-to-all-done.2.received = f32[128,32,128]{2,1,0:T(8,128)S(1)} async-done(((f32[128,32,128]{2,1,0:T(8,128)}), f32[128,32,128]{2,1,0:T(8,128)S(1)}, u32[]{:S(2)}, u32[]{:S(2)}) %all-to-all-start.2) | async-done | bytes 2097184 | tf_op jit(solution)/shard_map/all_to_all | solution.py:531
  67.1 3.5 %all-to-all-start.1 = ((f32[8,9,8,256]{3,2,1,0:T(8,128)}), f32[8,9,8,256]{3,2,1,0:T(8,128)S(1)}, u32[]{:S(2)}, u32[]{:S(2)}) async-start(f32[8,9,8,256]{3,2,1,0:T(8,128)} %rotate.2), calls=%async_computation.1 | async-start | bytes 1179648 | tf_op jit(solution)/shard_map/all_to_all | solution.py:497
  70.7 0.8 copy-done.3
  71.5 2.6 %edge.2 = f32[9,8,128]{2,1,0:T(8,128)} custom-call(f32[9,8,128]{2,1,0:T(8,128)} %get-tuple-element.16.column, f32[72,8,256]{2,1,0:T(8,128)} %copy-done.3, f32[72,8,256]{2,1,0:T(8,128)} %collective-permute-done.1.before, f32[2,8,256]{2,1,0:T(8,128)} %north.9, f32[2,8,256]{2,1,0:T(8,128)} %south.9), custom_call_target="tpu_custom_call" | custom-call | tf_op jit(solution)/shard_map/edge/pallas_call | solution.py:499
  74.1 4.1 %collective-permute-start.2 = (f32[9,8,128]{2,1,0:T(8,128)}, f32[9,8,128]{2,1,0:T(8,128)S(1)}, u32[]{:S(2)}, u32[]{:S(2)}) collective-permute-start(f32[9,8,128]{2,1,0:T(8,128)} %edge.2), channel_id=1, source_target_pairs={{0,112},{16,0},{32,16},{48,32},{64,48},{80,64},{96,80},{112,96},{1... | collective-permute-start | bytes 110600 | tf_op jit(solution)/shard_map/ppermute | solution.py:509
  78.1 13.8 %forcing.2.forced = f32[72,8,8,256]{3,2,1,0:T(8,128)} custom-call(f32[128,32,128]{2,1,0:T(8,128)} %copy-done), custom_call_target="tpu_custom_call" | custom-call | tf_op jit(solution)/shard_map/forcing/pallas_call | solution.py:177
  92.0 0.6 copy-done.8
  92.6 0.2 copy-done.4
  92.8 11.9 %middle.1 = (f32[72,8,8,256]{3,2,1,0:T(8,128)}, f32[72,8,256]{2,1,0:T(8,128)}, f32[72,8,256]{2,1,0:T(8,128)}, f32[8,10,8,256]{3,2,1,0:T(8,128)}, f32[9,8,128]{2,1,0:T(8,128)}, /*index=5*/f32[8,8,256]{2,1,0:T(8,128)}) custom-call(f32[72,8,8,256]{3,2,1,0:T(8,128)} %get-tuple-element.13.diffused, f32[72,8,256]{2,1,0:T(8,128)} %copy-done.3, ...), custom_call_target="tpu_custom_call" | custom-call | tf_op jit(solution)/shard_map/middle/pallas_call | solution.py:556
  104.7 3.5 %all-to-all-start.3 = ((f32[8,10,8,256]{3,2,1,0:T(8,128)}), f32[8,10,8,256]{3,2,1,0:T(8,128)S(1)}, u32[]{:S(2)}, u32[]{:S(2)}) async-start(f32[8,10,8,256]{3,2,1,0:T(8,128)} %get-tuple-element.22), calls=%async_computation.3 | async-start | bytes 1310720 | tf_op jit(solution)/shard_map/all_to_all | solution.py:484
  108.3 1.3 collective-permute-start.3
  109.6 3.1 %collective-permute-start.4 = (f32[72,8,256]{2,1,0:T(8,128)}, f32[72,8,256]{2,1,0:T(8,128)S(1)}, u32[]{:S(2)}, u32[]{:S(2)}) collective-permute-start(f32[72,8,256]{2,1,0:T(8,128)} %get-tuple-element.20), channel_id=1, source_target_pairs={{0,1},{1,2},{2,3},{3,4},{4,5},{5,6},{6,7},{7,8},{8,9},{9,10},{10,1... | collective-permute-start | bytes 1769480 | tf_op jit(solution)/shard_map/ppermute | solution.py:486
  112.6 5.2 %all-to-all-done.3.circle = f32[8,10,8,256]{3,2,1,0:T(8,128)S(1)} async-done(((f32[8,10,8,256]{3,2,1,0:T(8,128)}), f32[8,10,8,256]{3,2,1,0:T(8,128)S(1)}, u32[]{:S(2)}, u32[]{:S(2)}) %all-to-all-start.3) | async-done | bytes 655392 | tf_op jit(solution)/shard_map/all_to_all | solution.py:484
  117.9 0.8 copy-done.2
  118.7 5.9 %rotate.3 = f32[8,9,8,256]{3,2,1,0:T(8,128)} custom-call(s32[2,128]{1,0:T(2,128)} %shift.3, f32[8,10,8,256]{3,2,1,0:T(8,128)} %copy-done.2), custom_call_target="tpu_custom_call" | custom-call | tf_op jit(solution)/shard_map/rotate/pallas_call | solution.py:488
  124.6 3.5 %all-to-all-start.4 = ((f32[8,9,8,256]{3,2,1,0:T(8,128)}), f32[8,9,8,256]{3,2,1,0:T(8,128)S(1)}, u32[]{:S(2)}, u32[]{:S(2)}) async-start(f32[8,9,8,256]{3,2,1,0:T(8,128)} %rotate.3), calls=%async_computation.4 | async-start | bytes 1179648 | tf_op jit(solution)/shard_map/all_to_all | solution.py:497
  128.2 0.8 copy-done.5
  129.0 0.2 copy-done.6
  129.2 2.6 %edge.3 = f32[9,8,128]{2,1,0:T(8,128)} custom-call(f32[9,8,128]{2,1,0:T(8,128)} %get-tuple-element.21.column, f32[72,8,256]{2,1,0:T(8,128)} %copy-done.5, f32[72,8,256]{2,1,0:T(8,128)} %copy-done.6, f32[2,8,256]{2,1,0:T(8,128)} %north.9, f32[2,8,256]{2,1,0:T(8,128)} %south.9), custom_call_target="tpu_custom_call" | custom-call | tf_op jit(solution)/shard_map/edge/pallas_call | solution.py:499
  131.8 4.1 %collective-permute-start.5 = (f32[9,8,128]{2,1,0:T(8,128)}, f32[9,8,128]{2,1,0:T(8,128)S(1)}, u32[]{:S(2)}, u32[]{:S(2)}) collective-permute-start(f32[9,8,128]{2,1,0:T(8,128)} %edge.3), channel_id=1, source_target_pairs={{0,112},{16,0},{32,16},{48,32},{64,48},{80,64},{96,80},{112,96},{1... | collective-permute-start | bytes 110600 | tf_op jit(solution)/shard_map/ppermute | solution.py:509
  135.9 14.0 %forcing.3.forced = f32[72,8,8,256]{3,2,1,0:T(8,128)} custom-call(f32[128,32,128]{2,1,0:T(8,128)} %copy-done), custom_call_target="tpu_custom_call" | custom-call | tf_op jit(solution)/shard_map/forcing/pallas_call | solution.py:177
  149.9 0.6 copy-done.9
  150.7 10.2 %last.1 = (f32[72,8,8,256]{3,2,1,0:T(8,128)}, f32[8,8,256]{2,1,0:T(8,128)}) custom-call(f32[72,8,8,256]{3,2,1,0:T(8,128)} %get-tuple-element.18.diffused, f32[72,8,256]{2,1,0:T(8,128)} %copy-done.5, f32[72,8,256]{2,1,0:T(8,128)} %copy-done.6, f32[9,8,128]{2,1,0:T(8,128)} %copy-done.9, f32[8,9,8,256]{3,2,1,0:T(8,128)} %copy-done.7, f32[2,8,256]{2,1,0:T(8,128)} %north.9, ...), custom_call_target="tpu_custom_call" | custom-call | tf_op jit(solution)/shard_map/last/pallas_call | solution.py:576
  (23 shorter events, 0.3 us)
Async XLA Ops:
  0.6 15.4 %copy-start.10 = (s32[2,1]{0,1:T(1,128)S(1)}, s32[2,1]{0,1:T(1,128)}, u32[]{:S(2)}) copy-start(s32[2,1]{0,1:T(1,128)} %param.19) | copy-start | bytes 28
  9.7 17.1 %all-to-all-start = ((f32[8,10,8,256]{3,2,1,0:T(8,128)}), f32[8,10,8,256]{3,2,1,0:T(8,128)S(1)}, u32[]{:S(2)}, u32[]{:S(2)}) async-start(f32[8,10,8,256]{3,2,1,0:T(8,128)} %get-tuple-element.17), calls=%async_computation | async-start | bytes 1310720 | tf_op jit(solution)/shard_map/all_to_all | solution.py:484
  26.7 14.7 %copy-start.1 = (f32[8,10,8,256]{3,2,1,0:T(8,128)}, f32[8,10,8,256]{3,2,1,0:T(8,128)S(1)}, u32[]{:S(2)}) copy-start(f32[8,10,8,256]{3,2,1,0:T(8,128)S(1)} %all-to-all-done.circle) | copy-start | bytes 1966084
  26.7 40.4 %all-to-all-start.2 = ((f32[128,32,128]{2,1,0:T(8,128)}), f32[128,32,128]{2,1,0:T(8,128)S(1)}, u32[]{:S(2)}, u32[]{:S(2)}) async-start(f32[128,32,128]{2,1,0:T(8,128)} %pack.1), calls=%async_computation.2 | async-start | bytes 4194304 | tf_op jit(solution)/shard_map/all_to_all | solution.py:531
  36.2 34.4 %collective-permute-start = (f32[72,8,256]{2,1,0:T(8,128)}, f32[72,8,256]{2,1,0:T(8,128)S(1)}, u32[]{:S(2)}, u32[]{:S(2)}) collective-permute-start(f32[72,8,256]{2,1,0:T(8,128)} %get-tuple-element.14), channel_id=1, source_target_pairs={{1,0},{2,1},{3,2},{4,3},{5,4},{6,5},{7,6},{8,7},{9,8},{10,9},{11,1... | collective-permute-start | bytes 1769480 | tf_op jit(solution)/shard_map/ppermute | solution.py:485
  37.5 33.1 %collective-permute-start.1 = (f32[72,8,256]{2,1,0:T(8,128)}, f32[72,8,256]{2,1,0:T(8,128)}, u32[]{:S(2)}, u32[]{:S(2)}) collective-permute-start(f32[72,8,256]{2,1,0:T(8,128)} %get-tuple-element.15), channel_id=1, source_target_pairs={{0,1},{1,2},{2,3},{3,4},{4,5},{5,6},{6,7},{7,8},{8,9},{9,10},{10,1... | collective-permute-start | bytes 1769480 | tf_op jit(solution)/shard_map/ppermute | solution.py:486
  67.1 11.1 %copy-start = (f32[128,32,128]{2,1,0:T(8,128)}, f32[128,32,128]{2,1,0:T(8,128)S(1)}, u32[]{:S(2)}) copy-start(f32[128,32,128]{2,1,0:T(8,128)S(1)} %all-to-all-done.2.received) | copy-start | bytes 6291460
  67.1 24.9 %all-to-all-start.1 = ((f32[8,9,8,256]{3,2,1,0:T(8,128)}), f32[8,9,8,256]{3,2,1,0:T(8,128)S(1)}, u32[]{:S(2)}, u32[]{:S(2)}) async-start(f32[8,9,8,256]{3,2,1,0:T(8,128)} %rotate.2), calls=%async_computation.1 | async-start | bytes 1179648 | tf_op jit(solution)/shard_map/all_to_all | solution.py:497
  70.6 0.9 copy-start.3
  74.1 17.9 %collective-permute-start.2 = (f32[9,8,128]{2,1,0:T(8,128)}, f32[9,8,128]{2,1,0:T(8,128)S(1)}, u32[]{:S(2)}, u32[]{:S(2)}) collective-permute-start(f32[9,8,128]{2,1,0:T(8,128)} %edge.2), channel_id=1, source_target_pairs={{0,112},{16,0},{32,16},{48,32},{64,48},{80,64},{96,80},{112,96},{1... | collective-permute-start | bytes 110600 | tf_op jit(solution)/shard_map/ppermute | solution.py:509
  92.0 0.6 copy-start.8
  92.0 0.8 copy-start.4
  104.7 13.2 %all-to-all-start.3 = ((f32[8,10,8,256]{3,2,1,0:T(8,128)}), f32[8,10,8,256]{3,2,1,0:T(8,128)S(1)}, u32[]{:S(2)}, u32[]{:S(2)}) async-start(f32[8,10,8,256]{3,2,1,0:T(8,128)} %get-tuple-element.22), calls=%async_computation.3 | async-start | bytes 1310720 | tf_op jit(solution)/shard_map/all_to_all | solution.py:484
  108.3 19.9 %collective-permute-start.3 = (f32[72,8,256]{2,1,0:T(8,128)}, f32[72,8,256]{2,1,0:T(8,128)S(1)}, u32[]{:S(2)}, u32[]{:S(2)}) collective-permute-start(f32[72,8,256]{2,1,0:T(8,128)} %get-tuple-element.19), channel_id=1, source_target_pairs={{1,0},{2,1},{3,2},{4,3},{5,4},{6,5},{7,6},{8,7},{9,8},{10,9},{11,1... | collective-permute-start | bytes 1769480 | tf_op jit(solution)/shard_map/ppermute | solution.py:485
  109.6 18.6 %collective-permute-start.4 = (f32[72,8,256]{2,1,0:T(8,128)}, f32[72,8,256]{2,1,0:T(8,128)S(1)}, u32[]{:S(2)}, u32[]{:S(2)}) collective-permute-start(f32[72,8,256]{2,1,0:T(8,128)} %get-tuple-element.20), channel_id=1, source_target_pairs={{0,1},{1,2},{2,3},{3,4},{4,5},{5,6},{6,7},{7,8},{8,9},{9,10},{10,1... | collective-permute-start | bytes 1769480 | tf_op jit(solution)/shard_map/ppermute | solution.py:486
  117.9 0.8 copy-start.2
  124.6 25.3 %all-to-all-start.4 = ((f32[8,9,8,256]{3,2,1,0:T(8,128)}), f32[8,9,8,256]{3,2,1,0:T(8,128)S(1)}, u32[]{:S(2)}, u32[]{:S(2)}) async-start(f32[8,9,8,256]{3,2,1,0:T(8,128)} %rotate.3), calls=%async_computation.4 | async-start | bytes 1179648 | tf_op jit(solution)/shard_map/all_to_all | solution.py:497
  128.2 0.8 copy-start.5
  128.2 1.0 copy-start.6
  131.8 18.1 %collective-permute-start.5 = (f32[9,8,128]{2,1,0:T(8,128)}, f32[9,8,128]{2,1,0:T(8,128)S(1)}, u32[]{:S(2)}, u32[]{:S(2)}) collective-permute-start(f32[9,8,128]{2,1,0:T(8,128)} %edge.3), channel_id=1, source_target_pairs={{0,112},{16,0},{32,16},{48,32},{64,48},{80,64},{96,80},{112,96},{1... | collective-permute-start | bytes 110600 | tf_op jit(solution)/shard_map/ppermute | solution.py:509
  149.9 0.6 copy-start.9
  149.9 0.8 copy-start.7
